TPU v7x, 256 devices: a whole 4x4x8 slice. The times are simulated.
256 devices in a mesh: seq: 32 (over y, z), tp: 8 (over x, core).
Axes of the slice: x: 4, y: 4, z: 8, core: 2. Of those that a mesh axis runs over, the one named last changes fastest.
Arguments:
- values_in: bfloat16 [16384, 8192], P('seq', 'tp'), may hold values from -6 to 6
- gates_in: bfloat16 [16384, 8192], P('seq', 'tp'), may hold values from -6 to 6
- keys_in: bfloat16 [16384, 1024], P('seq', 'tp'), may hold values from -6 to 6
- queries_in: bfloat16 [16384, 1024], P('seq', 'tp'), may hold values from -6 to 6
- log_decay: float32 [128, 16384], P('tp', 'seq'), may hold values from -2 to 0, as said below
- conv_values: float32 [4, 8192], P(None, 'tp'), may hold values from -3 to 3
- bias_values: float32 [8192], P('tp'), may hold values from -3 to 3
- conv_keys: float32 [4, 1024], P(None, 'tp'), may hold values from -3 to 3
- bias_keys: float32 [1024], P('tp'), may hold values from -3 to 3
- conv_queries: float32 [4, 1024], P(None, 'tp'), may hold values from -3 to 3
- bias_queries: float32 [1024], P('tp'), may hold values from -3 to 3
- skip_scale: float32 [128], P('tp'), may hold values from 0.5 to 1.5
- norm_gain: float32 [8192], P('tp'), may hold values from 0.1 to 1.9
- out_weight: bfloat16 [8192, 4096], P('tp'), may hold values from -0.09375 to 0.09375
Outputs:
- mixer_out: bfloat16 [16384, 4096], P('seq', 'tp')
Inputs may be any that keep to these rules, and one draw needn't show every extreme that they name: `log_decay`: every entry is below zero.
All inputs are finite; a program needn't handle non-finite values.
Results may differ from a plain program's by a relative error of at most 0.015.
Values may be sent and summed in bfloat16 or wider, within the bound.
A program may use at most 64 MiB of HBM per device.

v0:
```python
from functools import partial
import jax
import jax.numpy as jnp
from jax import lax
from jax.sharding import PartitionSpec as P

N = 128
HIGH = lax.Precision.HIGHEST
norm_epsilon = 1e-05


def passed_along(block, axis, distance):
    devices = range(lax.axis_size(axis))
    route = [(i - distance, i) for i in devices if i - distance in devices]
    return lax.ppermute(block, axis, route)


def causal_filter(padded, kernel_weights, conv_bias, row_total):
    width = kernel_weights.shape[0]
    running = jnp.broadcast_to(conv_bias[None, :], (row_total, conv_bias.shape[0]))
    for offset in range(width):
        running = running + kernel_weights[offset][None, :] * padded[
            offset : offset + row_total
        ].astype(jnp.float32)
    return jax.nn.silu(running).astype(jnp.bfloat16)


def block_terms(carried, inputs, per_group):
    values, keys_block, queries, logs = inputs
    row_total = values.shape[0]
    groups = keys_block.shape[1]
    cumulative = jnp.cumsum(logs, axis=1)
    scores = jnp.einsum("tgn,sgn->gts", queries, keys_block, preferred_element_type=jnp.float32)
    positions = lax.broadcasted_iota(jnp.int32, (row_total, row_total), 0)
    sources = lax.broadcasted_iota(jnp.int32, (row_total, row_total), 1)
    log_gaps = jnp.where(
        (positions >= sources)[None], cumulative[:, :, None] - cumulative[:, None, :], -jnp.inf
    )
    mixing = (
        jnp.exp(log_gaps).reshape(groups, per_group, row_total, row_total) * scores[:, None]
    ).astype(jnp.bfloat16)
    local_part = jnp.einsum("ghts,sghp->tghp", mixing, values, preferred_element_type=jnp.float32)
    growth = jnp.exp(cumulative).T.reshape(row_total, groups, per_group, 1)
    from_state = (
        jnp.einsum("tgn,ghnp->tghp", queries.astype(jnp.float32), carried, precision=HIGH) * growth
    )
    remaining = jnp.exp(cumulative[:, -1:] - cumulative).T.reshape(row_total, groups, per_group, 1)
    weighted_keys = keys_block.astype(jnp.float32)[:, :, None, :] * remaining
    fresh_state = jnp.einsum(
        "tghn,tghp->ghnp", weighted_keys, values.astype(jnp.float32), precision=HIGH
    )
    carried = jnp.exp(cumulative[:, -1]).reshape(groups, per_group, 1, 1) * carried + fresh_state
    return (carried, local_part + from_state)


def shards(
    values_in,
    gates_in,
    keys_in,
    queries_in,
    log_decay,
    conv_values,
    bias_values,
    conv_keys,
    bias_keys,
    conv_queries,
    bias_queries,
    skip_scale,
    norm_gain,
    out_weight,
):
    row_total = values_in.shape[0]
    head_count = log_decay.shape[0]
    inner_width = values_in.shape[1]
    head_size = inner_width // head_count
    key_width = keys_in.shape[1]
    groups = key_width // N
    per_group = head_count // groups
    margin = conv_values.shape[0] - 1
    rim_send = jnp.concatenate(
        [
            values_in[row_total - margin :],
            keys_in[row_total - margin :],
            queries_in[row_total - margin :],
        ],
        axis=1,
    )
    rim_rows = passed_along(rim_send, "seq", 1)
    values = causal_filter(
        jnp.concatenate([rim_rows[:, :inner_width], values_in], axis=0),
        conv_values,
        bias_values,
        row_total,
    )
    keys_all = causal_filter(
        jnp.concatenate([rim_rows[:, inner_width : inner_width + key_width], keys_in], axis=0),
        conv_keys,
        bias_keys,
        row_total,
    )
    queries_all = causal_filter(
        jnp.concatenate([rim_rows[:, inner_width + key_width :], queries_in], axis=0),
        conv_queries,
        bias_queries,
        row_total,
    )
    block_rows = min(row_total, 512)
    block_count = row_total // block_rows
    value_blocks = values.reshape(block_count, block_rows, groups, per_group, head_size)
    key_blocks = keys_all.reshape(block_count, block_rows, groups, N)
    query_blocks = queries_all.reshape(block_count, block_rows, groups, N)
    log_blocks = log_decay.reshape(head_count, block_count, block_rows).transpose(1, 0, 2)
    initial = jnp.zeros((groups, per_group, N, head_size), jnp.float32)
    local_end, outputs = lax.scan(
        partial(block_terms, per_group=per_group),
        initial,
        (value_blocks, key_blocks, query_blocks, log_blocks),
    )
    cumulative = jnp.cumsum(log_decay, axis=1)
    device_log = cumulative[:, -1]
    flat_end = local_end.reshape(head_count, N * head_size)
    all_logs = lax.all_gather(device_log[None, :], "seq", axis=0, tiled=True)
    inclusive = jnp.cumsum(all_logs, axis=0)
    own_index = lax.axis_index("seq")
    before_mine = lax.dynamic_index_in_dim(inclusive - all_logs, own_index, 0, keepdims=False)
    pieces = lax.all_gather(flat_end[None].astype(jnp.bfloat16), "seq", axis=0, tiled=True).astype(
        jnp.float32
    )
    shard_ids = jnp.arange(pieces.shape[0], dtype=jnp.int32)
    through_shard = jnp.take(inclusive, shard_ids, axis=0)
    exponent = jnp.where(
        (shard_ids < own_index)[:, None], before_mine[None, :] - through_shard, -jnp.inf
    )
    incoming = jnp.zeros_like(flat_end) + jnp.einsum(
        "kh,khm->hm", jnp.exp(exponent), pieces, precision=HIGH
    )
    incoming = incoming.reshape(groups, per_group, N, head_size)
    growth = jnp.exp(cumulative).T.reshape(row_total, groups, per_group, 1)
    query_rows = queries_all.reshape(row_total, groups, N).astype(jnp.float32)
    from_before = jnp.einsum("tgn,ghnp->tghp", query_rows, incoming, precision=HIGH) * growth
    mixed = outputs.reshape(row_total, groups, per_group, head_size) + from_before
    mixed = mixed + skip_scale.reshape(groups, per_group)[None, :, :, None] * values.reshape(
        row_total, groups, per_group, head_size
    ).astype(jnp.float32)
    gated_rows = mixed.reshape(row_total, groups, per_group * head_size) * jax.nn.silu(
        gates_in.reshape(row_total, groups, per_group * head_size).astype(jnp.float32)
    )
    mean_square = jnp.mean(gated_rows * gated_rows, axis=-1, keepdims=True)
    normed = (
        (
            gated_rows
            * lax.rsqrt(mean_square + norm_epsilon)
            * norm_gain.reshape(groups, per_group * head_size)
        )
        .astype(jnp.bfloat16)
        .reshape(row_total, inner_width)
    )
    local_sum = jnp.dot(normed, out_weight, preferred_element_type=jnp.float32)
    summed = lax.psum(local_sum.astype(jnp.bfloat16), "tp").astype(jnp.float32)
    column_width = summed.shape[1] // lax.axis_size("tp")
    result = lax.dynamic_slice_in_dim(summed, lax.axis_index("tp") * column_width, column_width, 1)
    return result.astype(jnp.bfloat16)


def solution(mesh):
    placed = (
        P("seq", "tp"),
        P("seq", "tp"),
        P("seq", "tp"),
        P("seq", "tp"),
        P("tp", "seq"),
        P(None, "tp"),
        P("tp"),
        P(None, "tp"),
        P("tp"),
        P(None, "tp"),
        P("tp"),
        P("tp"),
        P("tp"),
        P("tp", None),
    )
    return jax.shard_map(
        shards, mesh=mesh, in_specs=placed, out_specs=P("seq", "tp"), check_vma=False
    )
```

profile of v0, /device:TPU:8, one launch (start us, length us, event | category | flops | bytes accessed | tf_op | source)
XLA Modules:
  0.0 248.3 jit_solution(196115072066289706)
XLA Ops:
  6.6 0.8 slice.96
  7.4 0.7 slice.97
  8.1 0.7 slice.98
  8.8 0.3 copy.48
  9.0 3.8 %collective-permute-start = (bf16[3,1280]{0,1:T(8,128)(2,1)S(1)}, bf16[3,1280]{0,1:T(8,128)(2,1)S(1)}, u32[]{:S(2)}, u32[]{:S(2)}) collective-permute-start(bf16[3,1280]{0,1:T(8,128)(2,1)S(1)} %copy.48), channel_id=1, source_target_pairs={{0,8},{8,16},{16,24},{24,32},{32,40},{40,48},{48,56},{56,64},{64,7... | collective-permute-start | bytes 23048 | tf_op jit(solution)/shard_map/ppermute | solution.py:15
  12.9 1.2 reduce-window.12
  14.5 0.9 fusion.41
  15.4 0.8 slice_bitcast_fusion.3
  16.3 1.5 copy.49
  17.8 6.5 %collective-permute-done = bf16[3,1280]{0,1:T(8,128)(2,1)S(1)} collective-permute-done((bf16[3,1280]{0,1:T(8,128)(2,1)S(1)}, bf16[3,1280]{0,1:T(8,128)(2,1)S(1)}, u32[]{:S(2)}, u32[]{:S(2)}) %collective-permute-start) | collective-permute-done | bytes 7712 | tf_op jit(solution)/shard_map/ppermute | solution.py:15
  24.7 2.7 %multiply_convert_fusion.3 = bf16[512,1024]{0,1:T(8,128)(2,1)S(1)} fusion(bf16[512,1024]{0,1:T(8,128)(2,1)S(1)} %copy.49, bf16[3,1024]{0,1:T(8,128)(2,1)S(1)} %slice.127, f32[1024]{0:T(1024)S(1)} %bitcast.91, f32[1024]{0:T(1024)S(1)} %bitcast.92, f32[1024]{0:T(1024)S(1)} %bitcast.90, f32[1024]{0:T(1024)S(1)} %bitcast.89, f32[1024]{0:T(1024)S(1)} %copy-done.7), kind=kLoop, calls=%fused_computation.25 | loop fusion | flops 13631488 | bytes 2123776 | tf_op jit(solution)/shard_map/convert_element_type | solution.py:25
  27.4 2.4 fusion.18
  29.9 0.3 copy.55
  30.1 1.2 convert_element_type.126
  31.4 0.6 dynamic-slice.1
  32.9 62.4 %all-reduce = f32[512]{0:T(512)S(1)} all-reduce(f32[512]{0:T(512)S(1)} %dynamic-update-slice), channel_id=2, replica_groups=mesh['seq'=32,'tp'=8] {'seq'}, use_global_device_ids=true, to_apply=%add | all-reduce | flops 512 | bytes 4096
  95.5 0.6 gather_fusion
  96.3 1.3 copy.57
  97.6 0.8 iota_compare_fusion
  98.7 0.3 fusion.42
  99.0 1.0 fusion.25
  100.0 5.8 %fusion.2 = f32[16,64,512]{2,1,0:T(8,128)} fusion(bf16[512,16,64]{0,2,1:T(8,128)(2,1)S(1)} %bitcast.86, f32[512,512]{1,0:T(8,128)S(1)} %fusion.42, f32[16,512]{1,0:T(8,128)S(1)} %copy_bitcast_fusion.1, pred[512,512]{1,0:T(8,128)(4,1)S(1)} %copy-done.4), kind=kOutput, calls=%fused_computation.4 | convolution fusion | flops 553648128 | bytes 4489216 | tf_op jit(solution)/shard_map/while/body/eval_jaxpr/ghts,sghp->tghp/dot_general | solution.py:42
  105.8 22.5 %all-gather.3.cloned.1.call-done = bf16[32,16,8192]{2,1,0:T(8,128)(2,1)} async-done(((bf16[1,16,8192]{2,1,0:T(8,128)(2,1)}), bf16[32,16,8192]{2,1,0:T(8,128)(2,1)}) %all-gather.3.cloned.1.call-update) | async-done | bytes 8388624 | tf_op jit(solution)/shard_map/all_gather | solution.py:126
  128.3 16.9 %fusion = f32[16,1,8192]{2,1,0:T(1,128)S(1)} fusion(f32[32,16,1]{0,2,1:T(1,128)S(1)} %copy.58, bf16[32,16,8192]{2,1,0:T(8,128)(2,1)} %all-gather.3.cloned.1.call-done), kind=kOutput, calls=%fused_computation.2 | convolution fusion | flops 50331648 | bytes 8914944 | tf_op jit(solution)/shard_map/kh,khm->hm/dot_general | solution.py:134
  145.2 1.1 copy.73
  146.3 2.5 reshape.210
  148.7 3.2 %fusion.31 = f32[16,64,512]{2,1,0:T(8,128)S(1)} fusion(f32[16,128,64]{2,1,0:T(8,128)} %reshape.210, bf16[512,128]{1,0:T(8,128)(2,1)S(1)} %multiply_convert_fusion.6), kind=kOutput, calls=%fused_computation.54 | convolution fusion | flops 805306368 | bytes 2752512 | tf_op jit(solution)/shard_map/tgn,ghnp->tghp/dot_general | solution.py:140
  152.0 1.0 fusion.10
  153.2 0.7 multiply_reduce_fusion
  153.9 9.7 %convolution_convert_fusion = bf16[512,4096]{1,0:T(8,128)(2,1)} fusion(bf16[1024,4096]{1,0:T(8,128)(2,1)} %param.27, f32[512,1024]{0,1:T(8,128)S(1)} %get-tuple-element.18, f32[1024]{0:T(1024)S(1)} %copy-done.12, f32[512]{0:T(512)S(1)} %add_rsqrt_fusion), kind=kOutput, calls=%fused_computation.6 | convolution fusion | flops 4298637312 | bytes 14686208 | tf_op jit(solution)/shard_map/dot_general | solution.py:158
  163.7 75.9 %all-reduce.3.cloned.1.call-done = bf16[512,4096]{1,0:T(8,128)(2,1)} async-done(((bf16[512,4096]{1,0:T(8,128)(2,1)}), bf16[512,4096]{1,0:T(8,128)(2,1)}) %all-reduce.3.cloned.1.call-update) | async-done | bytes 4194320 | tf_op jit(solution)/shard_map/psum | solution.py:159
  239.6 1.9 convert_convert_fusion
  (59 shorter events, 2.1 us)
Async XLA Ops:
  6.5 6.3 %copy-start = (f32[16,512]{1,0:T(8,128)S(1)}, f32[16,512]{1,0:T(8,128)}, u32[]{:S(2)}) copy-start(f32[16,512]{1,0:T(8,128)} %param.18) | copy-start | bytes 98308
  6.5 17.9 %copy-start.5 = (bf16[512,128]{1,0:T(8,128)(2,1)S(1)}, bf16[512,128]{1,0:T(8,128)(2,1)}, u32[]{:S(2)}) copy-start(bf16[512,128]{1,0:T(8,128)(2,1)} %param.16) | copy-start | bytes 393220
  6.5 17.9 %copy-start.9 = (f32[128]{0:T(128)S(1)}, f32[128]{0:T(128)}, u32[]{:S(2)}) copy-start(f32[128]{0:T(128)} %param.22) | copy-start | bytes 1540
  6.5 18.2 %copy-start.7 = (f32[1024]{0:T(1024)S(1)}, f32[1024]{0:T(1024)}, u32[]{:S(2)}) copy-start(f32[1024]{0:T(1024)} %param.20) | copy-start | bytes 12292
  6.5 121.8 %all-gather.3.cloned.1.call-start = ((), (), s32[]{:S(2)}) async-start(), calls=%async_computation | async-start | bytes 8650752 | tf_op jit(solution)/shard_map/all_gather | solution.py:126
  9.0 15.4 %collective-permute-start = (bf16[3,1280]{0,1:T(8,128)(2,1)S(1)}, bf16[3,1280]{0,1:T(8,128)(2,1)S(1)}, u32[]{:S(2)}, u32[]{:S(2)}) collective-permute-start(bf16[3,1280]{0,1:T(8,128)(2,1)S(1)} %copy.48), channel_id=1, source_target_pairs={{0,8},{8,16},{16,24},{24,32},{32,40},{40,48},{48,56},{56,64},{64,7... | collective-permute-start | bytes 23048 | tf_op jit(solution)/shard_map/ppermute | solution.py:15
  27.4 4.0 %copy-start.13 = (u32[256]{0:T(256)S(1)}, u32[256]{0:T(256)}, u32[]{:S(2)}) copy-start(u32[256]{0:T(256)} %constant.80) | copy-start | bytes 3076
  27.4 68.9 %copy-start.3 = (bf16[512,1024]{1,0:T(8,128)(2,1)S(1)}, bf16[512,1024]{1,0:T(8,128)(2,1)}, u32[]{:S(2)}) copy-start(bf16[512,1024]{1,0:T(8,128)(2,1)} %param.15) | copy-start | bytes 3145732
  29.8 68.6 %copy-start.8 = (f32[4,128]{1,0:T(4,128)S(1)}, f32[4,128]{1,0:T(4,128)}, u32[]{:S(2)}) copy-start(f32[4,128]{1,0:T(4,128)} %param.23) | copy-start | bytes 6148
  29.8 68.7 %copy-start.6 = (bf16[512,128]{1,0:T(8,128)(2,1)S(1)}, bf16[512,128]{1,0:T(8,128)(2,1)}, u32[]{:S(2)}) copy-start(bf16[512,128]{1,0:T(8,128)(2,1)} %param.17) | copy-start | bytes 393220
  29.8 68.7 %copy-start.10 = (f32[128]{0:T(128)S(1)}, f32[128]{0:T(128)}, u32[]{:S(2)}) copy-start(f32[128]{0:T(128)} %param.24) | copy-start | bytes 1540
  31.4 208.2 %all-reduce.3.cloned.1.call-start = ((), (), s32[]{:S(2)}) async-start(), calls=%async_computation.1 | async-start | bytes 8388608 | tf_op jit(solution)/shard_map/psum | solution.py:159
  98.5 1.5 copy-start.4
  146.3 5.7 %copy-start.11 = (f32[16]{0:T(128)S(1)}, f32[16]{0:T(128)}, u32[]{:S(2)}) copy-start(f32[16]{0:T(128)} %param.25) | copy-start | bytes 196
  148.7 3.2 %copy-start.2 = (f32[16,64,512]{2,1,0:T(8,128)S(1)}, f32[16,64,512]{2,1,0:T(8,128)}, u32[]{:S(2)}) copy-start(f32[16,64,512]{2,1,0:T(8,128)} %fusion.2) | copy-start | bytes 6291460
  152.0 1.2 copy-start.1
  153.2 0.7 copy-start.12
Sparse Core Ops, SparseCore 0:
  31.5 96.7 all-gather.2
  163.8 75.7 all-reduce.2
where the time goes:
time: 249 us; the launch traced here: 248 us
  waiting for transfers between devices  105 us (42%)
  blocking collectives  62.4 us (25%)
  matrix products  39.3 us (16%)
  local copies, waits for them, and re-layouts  14.4 us (6%)
  between operations  14.3 us (6%)
  other arithmetic  8.96 us (4%)
  starting transfers between devices  3.9 us (2%)
    psum x1, waiting for transfers between devices, shards(): summed = lax.psum(local_sum.astype(jnp.bfloat16), 'tp').astype(jnp.float32)  75.9 us
    unnamed x1, blocking collectives  62.4 us
    all_gather x1, waiting for transfers between devices, shards(): lax.all_gather(flat_end[None].astype(jnp.bfloat16), 'seq', axis=0, tiled=...  22.5 us
    dot_general x1, matrix products, shards(): jnp.einsum('kh,khm->hm', jnp.exp(exponent), pieces, precision=HIGH)  16.9 us
    dot_general x1, matrix products, shards(): local_sum = jnp.dot(normed, out_weight, preferred_element_type=jnp.float32)  9.74 us
    ppermute x1, waiting for transfers between devices, passed_along(): return lax.ppermute(block, axis, route)  6.53 us
    dot_general x1, matrix products, block_terms(): jnp.einsum('ghts,sghp->tghp', mixing, values, preferred_element_type=jnp....  5.8 us
  transfers between devices with their start and end apart: 3, of which 3 were waited for; matrix products, arithmetic and copies ran while one was open for 7% of the time, Pallas kernels for 0%

commit v1 on v0

--- a/solution.py
+++ b/solution.py
@@ -123,9 +123,12 @@
     inclusive = jnp.cumsum(all_logs, axis=0)
     own_index = lax.axis_index("seq")
     before_mine = lax.dynamic_index_in_dim(inclusive - all_logs, own_index, 0, keepdims=False)
-    pieces = lax.all_gather(flat_end[None].astype(jnp.bfloat16), "seq", axis=0, tiled=True).astype(
-        jnp.float32
-    )
+    pieces = jnp.concatenate(
+        lax.all_to_all(
+            jnp.stack([flat_end[None].astype(jnp.bfloat16)] * lax.axis_size("seq")), "seq", 0, 0
+        ),
+        axis=0,
+    ).astype(jnp.float32)
     shard_ids = jnp.arange(pieces.shape[0], dtype=jnp.int32)
     through_shard = jnp.take(inclusive, shard_ids, axis=0)
     exponent = jnp.where(

time: 249 us -> 420 us (1.69)
  blocking collectives: 62.4 us -> 239 us
  waiting for transfers between devices: 105 us -> 87.4 us
  starting transfers between devices: 3.9 us -> 13 us
    unnamed x1, blocking collectives: 62.4 us -> 239 us
    all_gather x1 -> x0, waiting for transfers between devices: 22.5 us -> none  [shards(): lax.all_gather(flat_end[None].astype(jnp.bfloat16), 'seq', axis=0, tiled=...]
    all_to_all x0 -> x1, starting transfers between devices: none -> 9.09 us  [shards(): lax.all_to_all(jnp.stack([flat_end[None].astype(jnp.bfloat16)] * lax.axis...]
    psum x1, waiting for transfers between devices: 75.9 us -> 80.9 us  [shards(): summed = lax.psum(local_sum.astype(jnp.bfloat16), 'tp').astype(jnp.float32)]
    another operation x4 -> x5, local copies, waits for them, and re-layouts: 2.61 us -> 6.84 us  [the longest x1 4.24 us: shards(): jnp.stack([flat_end[None].astype(jnp.bfloat16)] * lax.axis_size('seq'))]
  transfers between devices with their start and end apart: 3 -> 3, of which waited for: 3 -> 2; matrix products, arithmetic and copies ran while one was open for 7% -> 4% of each run, Pallas kernels for 0% -> 0%
where the time goes in v1:
time: 420 us; the launch traced here: 419 us
  blocking collectives  239 us (57%)
  waiting for transfers between devices  87.4 us (21%)
  matrix products  39.3 us (9%)
  local copies, waits for them, and re-layouts  17.9 us (4%)
  between operations  14.4 us (3%)
  starting transfers between devices  13 us (3%)
  other arithmetic  8.93 us (2%)
    unnamed x1, blocking collectives  239 us
    psum x1, waiting for transfers between devices, shards(): summed = lax.psum(local_sum.astype(jnp.bfloat16), 'tp').astype(jnp.float32)  80.9 us
    dot_general x1, matrix products, shards(): jnp.einsum('kh,khm->hm', jnp.exp(exponent), pieces, precision=HIGH)  16.9 us
    dot_general x1, matrix products, shards(): local_sum = jnp.dot(normed, out_weight, preferred_element_type=jnp.float32)  9.73 us
    all_to_all x1, starting transfers between devices, shards(): lax.all_to_all(jnp.stack([flat_end[None].astype(jnp.bfloat16)] * lax.axis...  9.09 us
  transfers between devices with their start and end apart: 3, of which 2 were waited for; matrix products, arithmetic and copies ran while one was open for 4% of the time, Pallas kernels for 0%

profile of v1, /device:TPU:8, one launch (start us, length us, event | category | flops | bytes accessed | tf_op | source)
XLA Modules:
  0.0 419.5 jit_solution(9266381358810345973)
XLA Ops:
  6.5 0.8 slice.96
  7.3 0.7 slice.97
  8.0 0.7 slice.98
  8.9 3.8 collective-permute-start
  12.8 1.2 reduce-window.12
  14.4 0.9 fusion.41
  15.3 0.8 slice_bitcast_fusion.3
  16.3 1.5 copy.49
  17.8 6.5 %collective-permute-done = bf16[3,1280]{0,1:T(8,128)(2,1)S(1)} collective-permute-done((bf16[3,1280]{0,1:T(8,128)(2,1)S(1)}, bf16[3,1280]{0,1:T(8,128)(2,1)S(1)}, u32[]{:S(2)}, u32[]{:S(2)}) %collective-permute-start) | collective-permute-done | bytes 7712 | tf_op jit(solution)/shard_map/ppermute | solution.py:15
  24.6 2.7 multiply_convert_fusion.3
  27.3 2.4 fusion.18
  29.7 0.3 copy.55
  30.0 0.5 convert_element_type.125
  30.5 4.2 %stack.2 = bf16[32,1,16,8192]{3,2,1,0:T(8,128)(2,1)} broadcast(bf16[16,8192]{1,0:T(8,128)(2,1)S(1)} %convert_element_type.125), dimensions={2,3} | broadcast | bytes 8650752 | tf_op jit(solution)/shard_map/stack | solution.py:128
  34.7 9.1 %all-to-all-start = ((bf16[32,1,16,8192]{3,2,1,0:T(8,128)(2,1)}), bf16[32,1,16,8192]{3,2,1,0:T(8,128)(2,1)}, u32[]{:S(2)}, u32[]{:S(2)}) async-start(bf16[32,1,16,8192]{3,2,1,0:T(8,128)(2,1)} %stack.2), calls=%async_computation | async-start | bytes 16777216 | tf_op jit(solution)/shard_map/all_to_all | solution.py:127
  43.9 0.6 dynamic-slice.1
  45.4 238.6 %all-reduce = f32[512]{0:T(512)S(1)} all-reduce(f32[512]{0:T(512)S(1)} %dynamic-update-slice), channel_id=2, replica_groups=mesh['seq'=32,'tp'=8] {'seq'}, use_global_device_ids=true, to_apply=%add | all-reduce | flops 512 | bytes 4096
  284.2 0.6 gather_fusion
  285.0 1.3 copy.57
  286.3 0.8 iota_compare_fusion
  287.4 0.3 fusion.42
  287.7 1.0 fusion.25
  288.7 5.8 %fusion.2 = f32[16,64,512]{2,1,0:T(8,128)} fusion(bf16[512,16,64]{0,2,1:T(8,128)(2,1)S(1)} %bitcast.87, f32[512,512]{1,0:T(8,128)S(1)} %fusion.42, f32[16,512]{1,0:T(8,128)S(1)} %copy_bitcast_fusion.1, pred[512,512]{1,0:T(8,128)(4,1)S(1)} %copy-done.4), kind=kOutput, calls=%fused_computation.4 | convolution fusion | flops 553648128 | bytes 4489216 | tf_op jit(solution)/shard_map/while/body/eval_jaxpr/ghts,sghp->tghp/dot_general | solution.py:42
  294.5 16.9 %fusion = f32[16,1,8192]{2,1,0:T(1,128)S(1)} fusion(f32[32,16,1]{0,2,1:T(1,128)S(1)} %copy.58, bf16[32,16,8192]{2,1,0:T(8,128)(2,1)} %bitcast.23), kind=kOutput, calls=%fused_computation.2 | convolution fusion | flops 50331648 | bytes 8914944 | tf_op jit(solution)/shard_map/kh,khm->hm/dot_general | solution.py:137
  311.4 1.1 copy.73
  312.5 2.4 reshape.213
  314.9 3.2 fusion.31
  318.2 1.0 fusion.10
  319.4 0.7 multiply_reduce_fusion
  320.1 9.7 %convolution_convert_fusion = bf16[512,4096]{1,0:T(8,128)(2,1)} fusion(bf16[1024,4096]{1,0:T(8,128)(2,1)} %param.27, f32[512,1024]{0,1:T(8,128)S(1)} %get-tuple-element.18, f32[1024]{0:T(1024)S(1)} %copy-done.12, f32[512]{0:T(512)S(1)} %add_rsqrt_fusion), kind=kOutput, calls=%fused_computation.6 | convolution fusion | flops 4298637312 | bytes 14686208 | tf_op jit(solution)/shard_map/dot_general | solution.py:161
  329.9 80.9 %all-reduce.3.cloned.1.call-done = bf16[512,4096]{1,0:T(8,128)(2,1)} async-done(((bf16[512,4096]{1,0:T(8,128)(2,1)}), bf16[512,4096]{1,0:T(8,128)(2,1)}) %all-reduce.3.cloned.1.call-update) | async-done | bytes 4194320 | tf_op jit(solution)/shard_map/psum | solution.py:162
  410.7 1.9 convert_convert_fusion
  (59 shorter events, 2.3 us)
Async XLA Ops:
  6.5 6.3 %copy-start = (f32[16,512]{1,0:T(8,128)S(1)}, f32[16,512]{1,0:T(8,128)}, u32[]{:S(2)}) copy-start(f32[16,512]{1,0:T(8,128)} %param.18) | copy-start | bytes 98308
  6.5 17.8 %copy-start.5 = (bf16[512,128]{1,0:T(8,128)(2,1)S(1)}, bf16[512,128]{1,0:T(8,128)(2,1)}, u32[]{:S(2)}) copy-start(bf16[512,128]{1,0:T(8,128)(2,1)} %param.16) | copy-start | bytes 393220
  6.5 17.9 %copy-start.9 = (f32[128]{0:T(128)S(1)}, f32[128]{0:T(128)}, u32[]{:S(2)}) copy-start(f32[128]{0:T(128)} %param.22) | copy-start | bytes 1540
  6.5 18.1 %copy-start.7 = (f32[1024]{0:T(1024)S(1)}, f32[1024]{0:T(1024)}, u32[]{:S(2)}) copy-start(f32[1024]{0:T(1024)} %param.20) | copy-start | bytes 12292
  8.9 15.4 %collective-permute-start = (bf16[3,1280]{0,1:T(8,128)(2,1)S(1)}, bf16[3,1280]{0,1:T(8,128)(2,1)S(1)}, u32[]{:S(2)}, u32[]{:S(2)}) collective-permute-start(bf16[3,1280]{0,1:T(8,128)(2,1)S(1)} %copy.48), channel_id=1, source_target_pairs={{0,8},{8,16},{16,24},{24,32},{32,40},{40,48},{48,56},{56,64},{64,7... | collective-permute-start | bytes 23048 | tf_op jit(solution)/shard_map/ppermute | solution.py:15
  34.7 9.2 %copy-start.13 = (u32[256]{0:T(256)S(1)}, u32[256]{0:T(256)}, u32[]{:S(2)}) copy-start(u32[256]{0:T(256)} %constant.80) | copy-start | bytes 3076
  34.7 250.2 %copy-start.3 = (bf16[512,1024]{1,0:T(8,128)(2,1)S(1)}, bf16[512,1024]{1,0:T(8,128)(2,1)}, u32[]{:S(2)}) copy-start(bf16[512,1024]{1,0:T(8,128)(2,1)} %param.15) | copy-start | bytes 3145732
  34.7 259.8 %all-to-all-start = ((bf16[32,1,16,8192]{3,2,1,0:T(8,128)(2,1)}), bf16[32,1,16,8192]{3,2,1,0:T(8,128)(2,1)}, u32[]{:S(2)}, u32[]{:S(2)}) async-start(bf16[32,1,16,8192]{3,2,1,0:T(8,128)(2,1)} %stack.2), calls=%async_computation | async-start | bytes 16777216 | tf_op jit(solution)/shard_map/all_to_all | solution.py:127
  43.8 243.3 %copy-start.8 = (f32[4,128]{1,0:T(4,128)S(1)}, f32[4,128]{1,0:T(4,128)}, u32[]{:S(2)}) copy-start(f32[4,128]{1,0:T(4,128)} %param.23) | copy-start | bytes 6148
  43.8 243.3 %copy-start.6 = (bf16[512,128]{1,0:T(8,128)(2,1)S(1)}, bf16[512,128]{1,0:T(8,128)(2,1)}, u32[]{:S(2)}) copy-start(bf16[512,128]{1,0:T(8,128)(2,1)} %param.17) | copy-start | bytes 393220
  43.8 243.3 %copy-start.10 = (f32[128]{0:T(128)S(1)}, f32[128]{0:T(128)}, u32[]{:S(2)}) copy-start(f32[128]{0:T(128)} %param.24) | copy-start | bytes 1540
  43.9 366.9 %all-reduce.3.cloned.1.call-start = ((), (), s32[]{:S(2)}) async-start(), calls=%async_computation.1 | async-start | bytes 8388608 | tf_op jit(solution)/shard_map/psum | solution.py:162
  287.2 1.5 copy-start.4
  312.5 5.7 %copy-start.11 = (f32[16]{0:T(128)S(1)}, f32[16]{0:T(128)}, u32[]{:S(2)}) copy-start(f32[16]{0:T(128)} %param.25) | copy-start | bytes 196
  314.9 3.2 copy-start.2
  318.2 1.2 copy-start.1
  319.4 0.7 copy-start.12
Sparse Core Ops, SparseCore 0:
  330.0 80.7 all-reduce.2
